TPU v7x, 512 devices: a whole 4x4x16 slice. The times are simulated.
512 devices in a mesh: pair: 16 (over y, z_lo), task: 32 (over z_hi, x, core).
Axes of the slice: x: 4, y: 4, z: 16 (z_hi: 4, z_lo: 4; z = z_hi * 4 + z_lo), core: 2. Of those that a mesh axis runs over, the one named last changes fastest.
Arguments:
- factor_blocks: bfloat16 [64, 1536, 625], P('task', 'pair'), may hold values from -1.25 to 1.25
- amplitudes: bfloat16 [64, 512, 625], P('task', 'pair'), may hold values from -0.15625 to 0.15625
- residual_in: float32 [64, 512, 625], P('task', 'pair'), may hold values from -6 to 6
- task_owners: int32 [512, 3], replicated, may hold values from 0 to 31, all different within a row; in each aligned block of 16 rows (0 to 15, 16 to 31, ...) at most 2 rows name the same one
- task_local: int32 [512, 4], replicated, may hold values from 0 to 1
Outputs:
- residual_out: float32 [64, 512, 625], P('task', 'pair')
Inputs may be any that keep to these rules, and one draw needn't show every extreme that they name: `task_owners`: the three numbers of a row differ; in each aligned block of 16 rows no number appears more than 2 times.
All inputs are finite; a program needn't handle non-finite values.
Results may differ from a plain program's by a relative error of at most 0.012.
Values may be sent and summed in bfloat16 or wider, within the bound.
A program may use at most 64 MiB of HBM per device.

v0:
```python
import jax
import jax.numpy as jnp
from jax import lax
from jax.sharding import PartitionSpec as P

TV = 25


def per_device(factor_blocks, amplitudes, residual_in, task_owners, task_local):
    pair_count = lax.axis_size("pair")
    task_count = lax.axis_size("task")
    helper = lax.axis_index("pair")
    column = lax.axis_index("task")
    blocks_here = factor_blocks.shape[0]
    tile_width = factor_blocks.shape[2]
    owners_all = task_owners.reshape(task_count, pair_count, 3)
    local_all = task_local.reshape(task_count, pair_count, 4)
    my_owners = lax.dynamic_index_in_dim(owners_all, column, 0, keepdims=False)
    my_local = lax.dynamic_index_in_dim(local_all, column, 0, keepdims=False)
    zero_value = jnp.zeros((), factor_blocks.dtype)
    factor_all, amps_all = (
        lax.all_gather(factor_blocks, "task", axis=0, tiled=True),
        lax.all_gather(amplitudes, "task", axis=0, tiled=True),
    )
    global_ids = my_owners * blocks_here + my_local[:, :3]
    factor_send = jnp.stack([factor_all[global_ids[:, 0]], factor_all[global_ids[:, 1]]], axis=0)
    amp_send = amps_all[global_ids[:, 2]][None]
    factor_recv, amp_recv = (
        lax.all_to_all(factor_send, "pair", split_axis=1, concat_axis=1, tiled=True),
        lax.all_to_all(amp_send, "pair", split_axis=1, concat_axis=1, tiled=True),
    )
    row_factor = factor_recv[0].reshape(-1, tile_width)
    col_factor = factor_recv[1].reshape(-1, tile_width)
    amp_block = amp_recv[0].reshape(-1, tile_width)
    integral_tile = lax.dot_general(
        row_factor, col_factor, (((0,), (0,)), ((), ())), preferred_element_type=jnp.float32
    ).astype(jnp.bfloat16)
    ladder = jnp.einsum(
        "icd,acbd->iab",
        amp_block.reshape(-1, TV, TV),
        integral_tile.reshape(TV, TV, TV, TV),
        preferred_element_type=jnp.float32,
    )
    ladder = ladder.astype(jnp.bfloat16).reshape(-1, tile_width)
    onehot = my_local[:, 3][None, :] == jnp.arange(blocks_here, dtype=jnp.int32)[:, None]
    my_target = lax.dynamic_index_in_dim(onehot, helper, 1, keepdims=False)
    partials = jnp.where(my_target[:, None, None], ladder[None], zero_value)
    block_sums = lax.psum_scatter(partials, "pair", scatter_dimension=1, tiled=True).astype(
        jnp.float32
    )
    return residual_in + block_sums


def solution(mesh):
    placed = (P("task", "pair", None), P("task", "pair", None), P("task", "pair", None), P(), P())
    return jax.shard_map(
        per_device, mesh=mesh, in_specs=placed, out_specs=P("task", "pair", None), check_vma=False
    )
```

profile of v0, /device:TPU:6, one launch (start us, length us, event | category | flops | bytes accessed | tf_op | source)
XLA Modules:
  0.0 456.4 jit_solution(9482900807218954983)
XLA Ops:
  6.5 0.0 all-gather.3.cloned.1.call-start
  6.5 0.7 all-gather.3.cloned.1.call-update
  7.3 0.0 all-gather.5.cloned.1.call-start
  7.3 0.7 all-gather.5.cloned.1.call-update
  8.0 0.8 reshape.21
  8.8 0.8 reshape.22
  9.7 88.0 %all-gather.3.cloned.1.call-done = bf16[64,32,625]{2,1,0:T(8,128)(2,1)} async-done(((bf16[2,32,625]{2,1,0:T(8,128)(2,1)}), bf16[64,32,625]{2,1,0:T(8,128)(2,1)}) %all-gather.3.cloned.1.call-update) | async-done | bytes 2560016 | tf_op jit(solution)/shard_map/all_gather | solution.py:23
  97.7 3.2 gather_fusion
  100.9 4.9 %all-to-all-start = ((bf16[1,16,32,625]{3,2,0,1:T(8,128)(2,1)}), bf16[1,16,32,625]{3,2,0,1:T(8,128)(2,1)S(1)}, u32[]{:S(2)}, u32[]{:S(2)}) async-start(bf16[1,16,32,625]{3,2,0,1:T(8,128)(2,1)} %bitcast.5), calls=%async_computation | async-start | bytes 1310720 | tf_op jit(solution)/shard_map/all_to_all | solution.py:30
  105.8 122.3 %all-gather.5.cloned.1.call-done = bf16[64,96,625]{2,1,0:T(8,128)(2,1)} async-done(((bf16[2,96,625]{2,1,0:T(8,128)(2,1)}), bf16[64,96,625]{2,1,0:T(8,128)(2,1)}) %all-gather.5.cloned.1.call-update) | async-done | bytes 7680016 | tf_op jit(solution)/shard_map/all_gather | solution.py:22
  228.1 4.1 gather_fusion.1
  232.2 5.4 %gather_fusion.2 = bf16[16,96,625]{2,1,0:T(8,128)(2,1)} fusion(bf16[64,96,625]{2,1,0:T(8,128)(2,1)} %all-gather.5.cloned.1.call-done, s32[1024]{0:T(1024)S(1)} %get-tuple-element.8), kind=kCustom, calls=%fused_computation.2 | custom fusion | bytes 3840064 | tf_op jit(solution)/shard_map/gather | solution.py:26
  237.6 2.1 pad_maximum_fusion
  239.7 2.5 copy.14
  242.2 0.0 all-to-all-done
  242.2 4.5 all-to-all-start.1
  246.7 0.2 reduce-scatter.2.cloned.1.call-start
  246.9 0.6 dynamic-slice
  247.5 0.7 compare_bitcast_fusion
  248.2 3.5 copy.13
  251.7 3.5 reshape.51
  255.2 83.1 %all-to-all-done.1 = bf16[2,16,96,625]{3,2,0,1:T(8,128)(2,1)} async-done(((bf16[2,16,96,625]{3,2,0,1:T(8,128)(2,1)}), bf16[2,16,96,625]{3,2,0,1:T(8,128)(2,1)}, u32[]{:S(2)}, u32[]{:S(2)}) %all-to-all-start.1) | async-done | bytes 3840032 | tf_op jit(solution)/shard_map/all_to_all | solution.py:29
  338.2 3.9 bitcast_convert_fusion.1
  342.1 0.0 copy-start
  342.1 12.5 %reshape.25 = bf16[25,25,25,25]{3,2,1,0:T(8,128)(2,1)} reshape(bf16[625,625]{1,0:T(8,128)(2,1)S(1)} %bitcast_convert_fusion.1) | data formatting | bytes 1562500 | tf_op jit(solution)/shard_map/reshape | solution.py:41
  354.6 0.0 copy-done
  354.6 3.6 bitcast_convert_fusion
  358.2 0.2 broadcast_in_dim.35
  358.4 0.3 copy.17
  358.7 0.0 copy-start.1
  358.7 1.3 broadcast_select_fusion
  360.0 0.0 reduce-scatter.2.cloned.1.call-update
  360.0 88.3 %reduce-scatter.2.cloned.1.call-done = bf16[2,32,625]{2,1,0:T(8,128)(2,1)} async-done(((bf16[2,512,625]{2,1,0:T(8,128)(2,1)}), bf16[2,32,625]{2,1,0:T(8,128)(2,1)}) %reduce-scatter.2.cloned.1.call-update) | async-done | bytes 80016 | tf_op jit(solution)/shard_map/reduce_scatter | solution.py:48
  448.3 0.0 copy-done.1
  448.3 1.6 convert_add_fusion
  (7 shorter events, 0.1 us)
Async XLA Ops:
  6.5 91.1 %all-gather.3.cloned.1.call-start = ((), (), s32[]{:S(2)}) async-start(), calls=%async_computation.3 | async-start | bytes 2703360 | tf_op jit(solution)/shard_map/all_gather | solution.py:23
  7.3 220.8 %all-gather.5.cloned.1.call-start = ((), (), s32[]{:S(2)}) async-start(), calls=%async_computation.4 | async-start | bytes 8110080 | tf_op jit(solution)/shard_map/all_gather | solution.py:22
  100.9 141.3 %all-to-all-start = ((bf16[1,16,32,625]{3,2,0,1:T(8,128)(2,1)}), bf16[1,16,32,625]{3,2,0,1:T(8,128)(2,1)S(1)}, u32[]{:S(2)}, u32[]{:S(2)}) async-start(bf16[1,16,32,625]{3,2,0,1:T(8,128)(2,1)} %bitcast.5), calls=%async_computation | async-start | bytes 1310720 | tf_op jit(solution)/shard_map/all_to_all | solution.py:30
  242.2 96.1 %all-to-all-start.1 = ((bf16[2,16,96,625]{3,2,0,1:T(8,128)(2,1)}), bf16[2,16,96,625]{3,2,0,1:T(8,128)(2,1)}, u32[]{:S(2)}, u32[]{:S(2)}) async-start(bf16[2,16,96,625]{3,2,0,1:T(8,128)(2,1)} %copy.14), calls=%async_computation.1 | async-start | bytes 7864320 | tf_op jit(solution)/shard_map/all_to_all | solution.py:29
  246.7 201.7 %reduce-scatter.2.cloned.1.call-start = ((), (), s32[]{:S(2)}) async-start(), calls=%async_computation.5 | async-start | bytes 1392640 | tf_op jit(solution)/shard_map/reduce_scatter | solution.py:48
  342.1 12.5 %copy-start = (bf16[512,25,25,1]{0,2,1,3:T(8,128)(2,1)S(1)}, bf16[512,25,25,1]{0,2,1,3:T(8,128)(2,1)}, u32[]{:S(2)}) copy-start(bf16[512,25,25,1]{0,2,1,3:T(8,128)(2,1)} %reshape.51) | copy-start | bytes 1920004
  358.7 89.6 %copy-start.1 = (f32[2,32,625]{2,1,0:T(8,128)S(1)}, f32[2,32,625]{2,1,0:T(8,128)}, u32[]{:S(2)}) copy-start(f32[2,32,625]{2,1,0:T(8,128)} %param.7) | copy-start | bytes 480004
Sparse Core Ops, SparseCore 0:
  10.5 87.1 all-gather.2
  100.8 127.2 all-gather.4
  360.1 88.1 reduce-scatter.1
where the time goes:
time: 457 us; the launch traced here: 456 us
  waiting for transfers between devices  383 us (84%)
  local copies, waits for them, and re-layouts  37.3 us (8%)
  between operations  13.3 us (3%)
  starting transfers between devices  9.65 us (2%)
  matrix products  7.46 us (2%)
  other arithmetic  5.64 us (1%)
    all_gather x1, waiting for transfers between devices, per_device(): lax.all_gather(factor_blocks, 'task', axis=0, tiled=True)  122 us
    reduce_scatter x1, waiting for transfers between devices, per_device(): lax.psum_scatter(partials, 'pair', scatter_dimension=1, tiled=True)  88.3 us
    all_gather x1, waiting for transfers between devices, per_device(): lax.all_gather(amplitudes, 'task', axis=0, tiled=True)  88 us
    all_to_all x1, waiting for transfers between devices, per_device(): lax.all_to_all(factor_send, 'pair', split_axis=1, concat_axis=1, tiled=True)  83.1 us
    reshape x1, local copies, waits for them, and re-layouts, per_device(): integral_tile.reshape(TV, TV, TV, TV)  12.5 us
  transfers between devices with their start and end apart: 5, of which 4 were waited for; matrix products, arithmetic and copies ran while one was open for 6% of the time, Pallas kernels for 0%

commit v1 on v0

v1 whole, which is shorter than its diff:
```python
import functools

import jax
import jax.numpy as jnp
from jax import lax
from jax.experimental import pallas as pl
from jax.experimental.pallas import tpu as pltpu
from jax.sharding import PartitionSpec as P

TV = 25
TT = 625
CH = 5
LN = 128
WIDE = CH * LN
STAGGER = 2.0
MESH = pl.DeviceIdType.MESH


def spread_matrix(swapped):
    k = lax.broadcasted_iota(jnp.int32, (TT, WIDE), 0)
    lane = lax.broadcasted_iota(jnp.int32, (TT, WIDE), 1)
    x = (k * 5243) >> 17
    y = k - x * TV
    if swapped:
        x, y = y, x
    group = (x * 13) >> 6
    target = group * LN + (x - group * 5) * TV + y
    return (lane == target).astype(jnp.float32).astype(jnp.bfloat16)


def kernel(
    base_ref, out_local_ref, factor_ref, amp_ref, residual_ref, out_ref,
    tiles, g0, g1, g2, g3, g4, s0, s1, s2, s3, s4, r0, r1, r2, r3, r4,
    v_ref, q_ref, w_ref, l_send, l_recv,
    spread_send, spread_recv, ring_send, ring_recv, plane_send, plane_recv, back_send, back_recv,
):
    gathered = (g0, g1, g2, g3, g4)
    sends = (s0, s1, s2, s3, s4)
    recvs = (r0, r1, r2, r3, r4)
    pair = lax.axis_index("pair")
    task = lax.axis_index("task")
    y, zl = pair // 4, pair % 4
    zh, x, core = task // 8, (task // 2) % 4, task % 2
    z = zh * 4 + zl

    def place(py, pz, px, pc):
        return {"pair": py * 4 + pz % 4, "task": ((pz // 4) * 4 + px) * 2 + pc}

    right = place(y, (z + 1) % 16, x, core)
    left = place(y, (z + 15) % 16, x, core)

    def plane_peer(n):
        return (y + n // 8) % 4, (x + (n // 2) % 4) % 4, (core + n % 2) % 2

    def column_peer(n):
        return (y + n // 4) % 4, (zl + n % 4) % 4

    barrier = pltpu.get_barrier_semaphore()

    @pl.loop(1, 32)
    def _(n):
        py, px, pc = plane_peer(n)
        pl.semaphore_signal(barrier, inc=1, device_id=place(py, z, px, pc), device_id_type=MESH)

    @pl.loop(1, 16)
    def _(n):
        py, pz = column_peer(n)
        pl.semaphore_signal(barrier, inc=1, device_id=place(py, zh * 4 + pz, x, core), device_id_type=MESH)

    pl.semaphore_signal(barrier, inc=1, device_id=right, device_id_type=MESH)
    pl.semaphore_signal(barrier, inc=1, device_id=left, device_id_type=MESH)

    spread = spread_matrix(False)
    for loc in range(2):
        rows = jnp.dot(factor_ref[loc], spread, preferred_element_type=jnp.float32).astype(jnp.bfloat16)
        for tile in range(6):
            for ch in range(CH):
                tiles[tile, ch, loc] = rows[tile * 16 : tile * 16 + 16, ch * LN : (ch + 1) * LN]
    swap = spread_matrix(True)
    for loc in range(2):
        rows = jnp.dot(amp_ref[loc], swap, preferred_element_type=jnp.float32).astype(jnp.bfloat16)
        for tile in range(2):
            for ch in range(CH):
                tiles[6 + tile, ch, loc] = rows[tile * 16 : tile * 16 + 16, ch * LN : (ch + 1) * LN]

    pl.semaphore_wait(barrier, 48)

    for ch in range(CH):
        for n in range(8):
            px, pc = (x + n // 2) % 4, (core + n % 2) % 2
            src = tiles.at[((px + 7 - zl) % 4) * 2 + pc, ch]
            dst = gathered[ch].at[pl.ds(z * 16 + (x * 2 + core) * 2, 2)]
            if n == 0:
                pltpu.make_async_copy(src, dst, spread_recv.at[ch]).start()
            else:
                pltpu.make_async_remote_copy(
                    src, dst, spread_send, spread_recv.at[ch], device_id=place(y, z, px, pc), device_id_type=MESH
                ).start()

    def slot(ch, zz, half=None):
        if half is None:
            return gathered[ch].at[pl.ds(zz * 16, 16)]
        return gathered[ch].at[pl.ds(zz * 16 + half * 8, 8)]

    def ring_copy(ch, side, step, zz):
        ref = slot(ch, zz, None if step < 7 else side)
        return pltpu.make_async_remote_copy(
            ref, ref, ring_send.at[ch], ring_recv.at[(ch * 2 + side) * 8 + step],
            device_id=right if side == 0 else left, device_id_type=MESH,
        )

    def ring(ch, step):
        if step == 0:
            own = slot(ch, z)
            pltpu.make_async_copy(own, own, spread_recv.at[ch]).wait()
        for side in range(2):
            zz = (z + 16 - step) % 16 if side == 0 else (z + step) % 16
            if step > 0:
                ring_copy(ch, side, step - 1, zz).wait_recv()
            if step < 8:
                ring_copy(ch, side, step, zz).start()

    def plane(ch):
        got, send, recv = gathered[ch], sends[ch], recvs[ch]

        @pl.loop(0, 32)
        def _(n):
            py, px, pc = plane_peer(n)
            k = ((zh * 4 + px) * 2 + pc) * 16 + py * 4 + zl
            row, col, amp = base_ref[k * 3], base_ref[k * 3 + 1], base_ref[k * 3 + 2]
            for r in range(3):
                at = ((x + 1 + r) % 4) * 16
                send[n, r] = got[row + at]
                send[n, 3 + r] = got[col + at]
            send[n, 6] = got[amp + x * 16]

        dst = recv.at[(y * 4 + x) * 2 + core]
        pltpu.make_async_copy(send.at[0], dst, plane_recv.at[ch]).start()

        @pl.loop(1, 32)
        def _(n):
            py, px, pc = plane_peer(n)
            pltpu.make_async_remote_copy(
                send.at[n], dst, plane_send.at[ch], plane_recv.at[ch],
                device_id=place(py, z, px, pc), device_id_type=MESH,
            ).start()

    def integrals(ch):
        recv = recvs[ch]
        pltpu.make_async_copy(recv, recv, plane_recv.at[ch]).wait()

        def rows_of(c, kb, first):
            return recvs[c][pl.ds(kb * 8, 8), first : first + 3].reshape(384, LN)

        for kb in range(4):
            row = rows_of(ch, kb, 0)
            cols = [rows_of(c, kb, 3) for c in range(ch + 1)]
            part = lax.dot_general(
                row, jnp.concatenate(cols, axis=1), (((0,), (0,)), ((), ())), preferred_element_type=jnp.float32
            )
            at = (slice(ch * LN, (ch + 1) * LN), slice(0, (ch + 1) * LN))
            v_ref[at] = part if kb == 0 else v_ref[at] + part
            if ch:
                before = jnp.concatenate([rows_of(c, kb, 0) for c in range(ch)], axis=1)
                part = lax.dot_general(
                    before, cols[-1], (((0,), (0,)), ((), ())), preferred_element_type=jnp.float32
                )
                at = (slice(0, ch * LN), slice(ch * LN, (ch + 1) * LN))
                v_ref[at] = part if kb == 0 else v_ref[at] + part

    events = []
    for ch in range(CH):
        for step in range(9):
            events.append((step + ch * STAGGER, ch, functools.partial(ring, ch, step)))
        events.append((8 + ch * STAGGER + 0.01, ch, functools.partial(plane, ch)))
        events.append((8 + ch * STAGGER + 5.0, ch, functools.partial(integrals, ch)))
    for _, _, event in sorted(events, key=lambda e: (e[0], e[1])):
        event()

    r = lax.broadcasted_iota(jnp.int32, (TV * 32, WIDE), 0)
    lane = lax.broadcasted_iota(jnp.int32, (TV * 32, WIDE), 1)
    d, b = r >> 5, r & 31
    group = (b * 13) >> 6
    target = jnp.where(b < TV, group * LN + (b - group * 5) * TV + d, -1)
    turn = (lane == target).astype(jnp.float32).astype(jnp.bfloat16)
    turned = lax.dot_general(
        turn, v_ref[...].astype(jnp.bfloat16), (((1,), (1,)), ((), ())), preferred_element_type=jnp.float32
    )
    q_ref[...] = turned.reshape(TV, 32, WIDE)

    lanes = lax.broadcasted_iota(jnp.int32, (32, LN), 1)

    @pl.loop(0, CH)
    def _(i):
        lane_i = pl.ds(pl.multiple_of(i * LN, LN), LN)
        for g in range(CH):
            src = [q_ref[g * 5 + dd, :, lane_i] for dd in range(5)]
            for aa in range(5):
                acc = jnp.zeros((32, LN), jnp.float32)
                for dd in range(5):
                    shift = ((dd - aa) * TV) % LN
                    moved = pltpu.roll(src[dd], shift, 1) if shift else src[dd]
                    acc = jnp.where((lanes >= dd * TV) & (lanes < (dd + 1) * TV), moved, acc)
                count = TV if aa < 4 else 28
                w_ref[i, aa * TV : aa * TV + count, g * LN : (g + 1) * LN] = acc[:count]

    amps = jnp.concatenate([recvs[c][:, 6].reshape(512, LN) for c in range(CH)], axis=1)
    for i in range(CH):
        ladder = lax.dot_general(
            amps, w_ref[i].astype(jnp.bfloat16), (((1,), (1,)), ((), ())), preferred_element_type=jnp.float32
        )
        l_send[:, i] = ladder.astype(jnp.bfloat16).reshape(16, 32, LN)

    l_dst = l_recv.at[pair]
    pltpu.make_async_copy(l_send.at[pair], l_dst, back_recv).start()

    @pl.loop(1, 16)
    def _(n):
        py, pz = column_peer(n)
        pltpu.make_async_remote_copy(
            l_send.at[py * 4 + pz], l_dst, back_send, back_recv,
            device_id=place(py, zh * 4 + pz, x, core), device_id_type=MESH,
        ).start()

    part = tiles.at[pl.ds(0, 7)]
    pltpu.make_async_copy(part, part, spread_send).wait()
    for ch in range(CH):
        part = gathered[ch].at[pl.ds(0, 240)]
        pltpu.make_async_copy(part, part, ring_send.at[ch]).wait()
        part = sends[ch].at[pl.ds(0, 31)]
        pltpu.make_async_copy(part, part, plane_send.at[ch]).wait()

    pltpu.make_async_copy(l_recv, l_recv, back_recv).wait()
    for i in range(CH):
        sums = [jnp.zeros((32, LN), jnp.float32) for _ in range(2)]
        for src in range(16):
            tile = l_recv[src, i].astype(jnp.float32)
            here = out_local_ref[task * 16 + src]
            sums = [sums[loc] + jnp.where(here == loc, tile, 0.0) for loc in range(2)]
        for loc in range(2):
            v_ref[loc * 32 : loc * 32 + 32, i * LN : (i + 1) * LN] = sums[loc]
    for loc in range(2):
        total = v_ref[loc * 32 : loc * 32 + 32, :]
        joined = jnp.concatenate([total[:, i * LN : i * LN + 125] for i in range(CH)], axis=1)
        out_ref[loc] = residual_ref[loc] + joined
    part = l_send.at[pl.ds(0, 15)]
    pltpu.make_async_copy(part, part, back_send).wait()


def per_device(factor_blocks, amplitudes, residual_in, task_owners, task_local):
    ids = task_owners * 2 + task_local[:, :3]
    base = ((ids // 16) * 64 + ids % 16).reshape(-1)
    out_local = task_local[:, 3]
    vmem = pl.BlockSpec(memory_space=pltpu.VMEM)
    smem = pl.BlockSpec(memory_space=pltpu.SMEM)
    bf16, f32 = jnp.bfloat16, jnp.float32
    dma = pltpu.SemaphoreType.DMA
    return pl.pallas_call(
        kernel,
        out_shape=jax.ShapeDtypeStruct(residual_in.shape, residual_in.dtype),
        in_specs=[smem, smem, vmem, vmem, vmem],
        out_specs=vmem,
        scratch_shapes=[pltpu.VMEM((8, CH, 2, 16, LN), bf16)]
        + [pltpu.VMEM((256, 16, LN), bf16)] * CH
        + [pltpu.VMEM((32, 7, 16, LN), bf16)] * (2 * CH)
        + [
            pltpu.VMEM((WIDE, WIDE), f32),
            pltpu.VMEM((TV, 32, WIDE), f32),
            pltpu.VMEM((CH, LN, WIDE), f32),
            pltpu.VMEM((16, CH, 32, LN), bf16),
            pltpu.VMEM((16, CH, 32, LN), bf16),
            dma,
            dma((CH,)),
            dma((CH,)),
            dma((CH * 16,)),
            dma((CH,)),
            dma((CH,)),
            dma,
            dma,
        ],
        compiler_params=pltpu.CompilerParams(collective_id=0, has_side_effects=True),
    )(base, out_local, factor_blocks, amplitudes, residual_in)


def solution(mesh):
    placed = (P("task", "pair", None), P("task", "pair", None), P("task", "pair", None), P(), P())
    return jax.shard_map(
        per_device, mesh=mesh, in_specs=placed, out_specs=P("task", "pair", None), check_vma=False
    )
```

time: 457 us -> 137 us (0.30)
  waiting for transfers between devices: 383 us -> 0 us
  Pallas kernels: 0 us -> 130 us
  local copies, waits for them, and re-layouts: 37.3 us -> 3.81 us
  between operations: 13.3 us -> 0.02 us
  starting transfers between devices: 9.65 us -> 0 us
  matrix products: 7.46 us -> 0 us
  other arithmetic: 5.64 us -> 0.74 us
    all_gather x2 -> x0, waiting for transfers between devices: 210 us -> none  [the longest x1 122 us: per_device(): lax.all_gather(factor_blocks, 'task', axis=0, tiled=True)]
    pallas_call x0 -> x1, Pallas kernels: none -> 130 us  [per_device(): pl.pallas_call(kernel, out_shape=jax.ShapeDtypeStruct(residual_in.shape,...]
    reduce_scatter x1 -> x0, waiting for transfers between devices: 88.3 us -> none  [per_device(): lax.psum_scatter(partials, 'pair', scatter_dimension=1, tiled=True)]
    all_to_all x2 -> x0, waiting for transfers between devices: 83.1 us -> none  [the longest x1 83.1 us: per_device(): lax.all_to_all(factor_send, 'pair', split_axis=1, concat_axis=1, tiled=True)]
    reshape x3 -> x1, local copies, waits for them, and re-layouts: 14 us -> 0.81 us  [per_device(): base = (ids // 16 * 64 + ids % 16).reshape(-1)]
    gather x3 -> x0, local copies, waits for them, and re-layouts: 12.7 us -> none  [the longest x1 5.37 us: per_device(): factor_all[global_ids[:, 1]]]
    all_to_all x2 -> x0, starting transfers between devices: 9.39 us -> none  [the longest x1 4.88 us: per_device(): lax.all_to_all(amp_send, 'pair', split_axis=1, concat_axis=1, tiled=True)]
    dot_general x2 -> x0, matrix products: 7.46 us -> none  [the longest x1 3.86 us: per_device(): lax.dot_general(row_factor, col_factor, (((0,), (0,)), ((), ())), preferr...]
  transfers between devices with their start and end apart: 5 -> 0, of which waited for: 4 -> 0; matrix products, arithmetic and copies ran while one was open for 6% -> 0% of each run, Pallas kernels for 0% -> 0%
where the time goes in v1:
time: 137 us; the launch traced here: 134 us
  Pallas kernels  130 us (95%)
  local copies, waits for them, and re-layouts  3.81 us (3%)
    pallas_call x1, Pallas kernels, per_device(): pl.pallas_call(kernel, out_shape=jax.ShapeDtypeStruct(residual_in.shape,...  130 us

profile of v1, /device:TPU:6, one launch (start us, length us, event | category | flops | bytes accessed | tf_op | source)
XLA Modules:
  0.0 134.4 jit_solution(9399576005748893554)
XLA Ops:
  0.0 1.3 slice.7
  1.3 0.7 fusion.1
  2.0 0.1 copy.6
  2.2 0.8 reshape.3.base_ref
  3.0 129.9 %shard_map.55 = f32[2,32,625]{2,1,0:T(8,128)} custom-call(s32[1536]{0:T(1024)} %reshape.3.base_ref, s32[512]{0:T(512)} %bitcast.1, bf16[2,96,625]{2,1,0:T(8,128)(2,1)} %factor_ref.1, bf16[2,32,625]{2,1,0:T(8,128)(2,1)} %amp_ref.1, f32[2,32,625]{2,1,0:T(8,128)} %residual_ref.1), custom_call_target="tpu_custom_call" | custom-call | tf_op jit(solution)/shard_map/pallas_call | solution.py:258
  132.8 1.6 %copy.8 = f32[2,32,625]{2,1,0:T(8,128)} copy(f32[2,32,625]{2,1,0:T(8,128)} %shard_map.55) | data formatting | bytes 320000

commit v2 on v1

v2 whole, which is shorter than its diff:
```python
import functools

import jax
import jax.numpy as jnp
from jax import lax
from jax.experimental import pallas as pl
from jax.experimental.pallas import tpu as pltpu
from jax.sharding import PartitionSpec as P

TV = 25
TT = 625
CH = 5
LN = 128
WIDE = CH * LN
MESH = pl.DeviceIdType.MESH
HALF_US = 0.72
HOP_US = 2.2
READY_US = 0.7


def ring_order():
    ready = {(ch, half): ch * READY_US for ch in range(CH) for half in range(2)}
    step = {key: 0 for key in ready}
    order, now = [], 0.0
    while ready:
        now = max(now, min(ready.values()))
        key = min((k for k in ready if ready[k] <= now), key=lambda k: (24 + 8.3 * k[0] - (8 - step[k]) * 2.9, k))
        order.append((now, key, step[key]))
        at = step[key]
        step[key] += 1
        if at == 8:
            del ready[key]
            continue
        now += HALF_US if at < 7 else HALF_US / 2
        ready[key] = now + HOP_US
    return order


def swap_matrix():
    k = lax.broadcasted_iota(jnp.int32, (TT, WIDE), 0)
    lane = lax.broadcasted_iota(jnp.int32, (TT, WIDE), 1)
    c = (k * 5243) >> 17
    d = k - c * TV
    group = (d * 13) >> 6
    target = group * LN + (d - group * 5) * TV + c
    return (lane == target).astype(jnp.float32).astype(jnp.bfloat16)


def turn_matrix():
    r = lax.broadcasted_iota(jnp.int32, (TV * 32, WIDE), 0)
    lane = lax.broadcasted_iota(jnp.int32, (TV * 32, WIDE), 1)
    d, b = r >> 5, r & 31
    group = (b * 13) >> 6
    target = jnp.where(b < TV, group * LN + (b - group * 5) * TV + d, -1)
    return (lane == target).astype(jnp.float32).astype(jnp.bfloat16)


def kernel(
    owners_ref, local_ref, factor_hbm, amp_hbm, residual_hbm, out_ref,
    factor_ref, amp_ref, residual_ref, base_ref, turn_ref,
    tiles, g0, g1, g2, g3, g4, s0, s1, s2, s3, s4, r0, r1, r2, r3, r4,
    v_ref, q_ref, w_ref, l_send, l_recv, sum_ref,
    load_sem, spread_send, spread_recv, ring_send, ring_recv, plane_send, plane_recv, back_send, back_recv,
):
    gathered = (g0, g1, g2, g3, g4)
    sends = (s0, s1, s2, s3, s4)
    recvs = (r0, r1, r2, r3, r4)
    loads = [
        pltpu.make_async_copy(src, dst, load_sem.at[i])
        for i, (src, dst) in enumerate(
            ((factor_hbm, factor_ref), (amp_hbm, amp_ref), (residual_hbm, residual_ref))
        )
    ]
    for load in loads:
        load.start()

    pair = lax.axis_index("pair")
    task = lax.axis_index("task")
    y, zl = pair // 4, pair % 4
    zh, x, core = task // 8, (task // 2) % 4, task % 2
    z = zh * 4 + zl

    def place(py, pz, px, pc):
        return {"pair": py * 4 + pz % 4, "task": ((pz // 4) * 4 + px) * 2 + pc}

    right = place(y, (z + 1) % 16, x, core)
    left = place(y, (z + 15) % 16, x, core)

    def plane_peer(n):
        n = (n * 5) % 32
        return (y + n // 8) % 4, (x + (n // 2) % 4) % 4, (core + n % 2) % 2

    def column_peer(n):
        return (y + n // 4) % 4, (zl + n % 4) % 4

    barrier = pltpu.get_barrier_semaphore()

    @pl.loop(1, 32)
    def _(n):
        py, px, pc = plane_peer(n)
        pl.semaphore_signal(barrier, inc=1, device_id=place(py, z, px, pc), device_id_type=MESH)

    @pl.loop(1, 16)
    def _(n):
        py, pz = column_peer(n)
        pl.semaphore_signal(barrier, inc=1, device_id=place(py, zh * 4 + pz, x, core), device_id_type=MESH)

    pl.semaphore_signal(barrier, inc=1, device_id=right, device_id_type=MESH)
    pl.semaphore_signal(barrier, inc=1, device_id=left, device_id_type=MESH)

    swap = swap_matrix()
    loads[0].wait()
    for loc in range(2):
        for ch in range(CH):
            rows = factor_ref[loc, :, ch * 125 : ch * 125 + 125]
            rows = jnp.concatenate([rows, jnp.zeros((96, 3), jnp.bfloat16)], axis=1)
            tiles[0:6, ch, loc] = rows.reshape(6, 16, LN)
    loads[1].wait()
    for loc in range(2):
        rows = jnp.dot(amp_ref[loc], swap, preferred_element_type=jnp.float32).astype(jnp.bfloat16)
        for ch in range(CH):
            tiles[6:8, ch, loc] = rows[:, ch * LN : (ch + 1) * LN].reshape(2, 16, LN)

    pl.semaphore_wait(barrier, 48)

    for ch in range(CH):
        for n in range(8):
            px, pc = (x + n // 2) % 4, (core + n % 2) % 2
            src = tiles.at[((px + 7 - zl) % 4) * 2 + pc, ch]
            dst = gathered[ch].at[pl.ds(z * 16 + (x * 2 + core) * 2, 2)]
            if n == 0:
                pltpu.make_async_copy(src, dst, spread_recv.at[ch]).start()
            else:
                pltpu.make_async_remote_copy(
                    src, dst, spread_send, spread_recv.at[ch], device_id=place(y, z, px, pc), device_id_type=MESH
                ).start()

    @pl.loop(0, 32)
    def _(n):
        py, px, pc = plane_peer(n)
        k = ((zh * 4 + px) * 2 + pc) * 16 + py * 4 + zl
        for i in range(3):
            m = owners_ref[i, k] * 2 + local_ref[i, k]
            base_ref[n * 3 + i] = (m // 16) * 64 + m % 16

    def half_slot(ch, zz, half):
        return gathered[ch].at[pl.ds(zz * 16 + half * 8, 8)]

    def ring_copy(ch, half, side, step, zz):
        ref = half_slot(ch, zz, half)
        return pltpu.make_async_remote_copy(
            ref, ref, ring_send.at[ch], ring_recv.at[((ch * 2 + half) * 2 + side) * 8 + step],
            device_id=right if side == 0 else left, device_id_type=MESH,
        )

    spread_done = [False] * CH

    def ring(ch, half, step):
        if step == 0 and not spread_done[ch]:
            own = gathered[ch].at[pl.ds(z * 16, 16)]
            pltpu.make_async_copy(own, own, spread_recv.at[ch]).wait()
            spread_done[ch] = True
        for side in range(2):
            zz = (z + 16 - step) % 16 if side == 0 else (z + step) % 16
            if 0 < step < 8 or (step == 8 and side == half):
                ring_copy(ch, half, side, step - 1, zz).wait_recv()
            if step < 7 or (step == 7 and side == half):
                ring_copy(ch, half, side, step, zz).start()

    def plane(ch):
        got, send, recv = gathered[ch], sends[ch], recvs[ch]
        dst = recv.at[(y * 4 + x) * 2 + core]

        @pl.loop(0, 32)
        def _(n):
            row, col, amp = base_ref[n * 3], base_ref[n * 3 + 1], base_ref[n * 3 + 2]
            for r in range(3):
                at = ((x + 1 + r) % 4) * 16
                send[n, r] = got[row + at]
                send[n, 3 + r] = got[col + at]
            send[n, 6] = got[amp + x * 16]

        pltpu.make_async_copy(send.at[0], dst, plane_recv.at[ch]).start()

        @pl.loop(1, 32)
        def _(n):
            py, px, pc = plane_peer(n)
            pltpu.make_async_remote_copy(
                send.at[n], dst, plane_send.at[ch], plane_recv.at[ch],
                device_id=place(py, z, px, pc), device_id_type=MESH,
            ).start()

    def integrals(ch, kb):
        recv = recvs[ch]
        if kb == 0:
            pltpu.make_async_copy(recv, recv, plane_recv.at[ch]).wait()

        def rows_of(c, first):
            return recvs[c][pl.ds(kb * 8, 8), first : first + 3].reshape(384, LN)

        row = rows_of(ch, 0)
        cols = [rows_of(c, 3) for c in range(ch + 1)]
        part = lax.dot_general(
            row, jnp.concatenate(cols, axis=1), (((0,), (0,)), ((), ())), preferred_element_type=jnp.float32
        )
        at = (slice(ch * LN, (ch + 1) * LN), slice(0, (ch + 1) * LN))
        v_ref[at] = part if kb == 0 else v_ref[at] + part
        if ch:
            before = jnp.concatenate([rows_of(c, 0) for c in range(ch)], axis=1)
            part = lax.dot_general(before, cols[-1], (((0,), (0,)), ((), ())), preferred_element_type=jnp.float32)
            at = (slice(0, ch * LN), slice(ch * LN, (ch + 1) * LN))
            v_ref[at] = part if kb == 0 else v_ref[at] + part

    def make_turn():
        turn_ref[...] = turn_matrix()

    PLANE_US = 10.0
    order = ring_order()
    events = [(t, functools.partial(ring, ch, half, step)) for t, (ch, half), step in order]
    free = 0.0
    for ch in range(CH):
        done = max(t for t, (c, _), step in order if c == ch and step == 8)
        events.append((done + 1e-4, functools.partial(plane, ch)))
        free = max(free, done) + PLANE_US
        for kb in range(4):
            events.append((free + 4.0 + kb * 1.5, functools.partial(integrals, ch, kb)))
    events.append((8.0, make_turn))
    for _, event in sorted(events, key=lambda e: e[0]):
        event()

    amps = jnp.concatenate([recvs[c][:, 6].reshape(512, LN) for c in range(CH)], axis=1)
    lanes = lax.broadcasted_iota(jnp.int32, (32, LN), 1)

    @pl.loop(0, CH)
    def _(i):
        part = v_ref[pl.ds(pl.multiple_of(i * LN, LN), LN), :].astype(jnp.bfloat16)
        turned = lax.dot_general(turn_ref[...], part, (((1,), (1,)), ((), ())), preferred_element_type=jnp.float32)
        q_ref[...] = turned.reshape(TV, 32, LN)
        for g in range(CH):
            src = [q_ref[g * 5 + dd] for dd in range(5)]
            for aa in range(5):
                acc = jnp.zeros((32, LN), jnp.float32)
                for dd in range(5):
                    shift = ((dd - aa) * TV) % LN
                    moved = pltpu.roll(src[dd], shift, 1) if shift else src[dd]
                    acc = jnp.where((lanes >= dd * TV) & (lanes < (dd + 1) * TV), moved, acc)
                count = TV if aa < 4 else 28
                w_ref[aa * TV : aa * TV + count, g * LN : (g + 1) * LN] = acc[:count]
        ladder = lax.dot_general(
            amps, w_ref[...].astype(jnp.bfloat16), (((1,), (1,)), ((), ())), preferred_element_type=jnp.float32
        )
        l_send[i] = ladder.astype(jnp.bfloat16).reshape(16, 32, LN)
        dst = l_recv.at[i, pair]
        pltpu.make_async_copy(l_send.at[i, pair], dst, back_recv.at[i]).start()

        @pl.loop(1, 16)
        def _(n):
            py, pz = column_peer(n)
            pltpu.make_async_remote_copy(
                l_send.at[i, py * 4 + pz], dst, back_send, back_recv.at[i],
                device_id=place(py, zh * 4 + pz, x, core), device_id_type=MESH,
            ).start()

    part = tiles.at[pl.ds(0, 7)]
    pltpu.make_async_copy(part, part, spread_send).wait()
    for ch in range(CH):
        part = gathered[ch].at[pl.ds(0, 240)]
        pltpu.make_async_copy(part, part, ring_send.at[ch]).wait()
        part = sends[ch].at[pl.ds(0, 31)]
        pltpu.make_async_copy(part, part, plane_send.at[ch]).wait()

    loads[2].wait()
    for i in range(CH):
        pltpu.make_async_copy(l_recv.at[i], l_recv.at[i], back_recv.at[i]).wait()
        sums = [jnp.zeros((32, LN), jnp.float32) for _ in range(2)]
        for src in range(16):
            tile = l_recv[i, src].astype(jnp.float32)
            here = local_ref[3, task * 16 + src]
            sums = [sums[loc] + jnp.where(here == loc, tile, 0.0) for loc in range(2)]
        for loc in range(2):
            sum_ref[loc, :, i * LN : (i + 1) * LN] = sums[loc]
    for loc in range(2):
        joined = jnp.concatenate([sum_ref[loc, :, i * LN : i * LN + 125] for i in range(CH)], axis=1)
        out_ref[loc] = residual_ref[loc] + joined
    part = l_send.at[:, pl.ds(0, 15)]
    pltpu.make_async_copy(part, part, back_send).wait()


def per_device(factor_blocks, amplitudes, residual_in, task_owners, task_local):
    vmem = pl.BlockSpec(memory_space=pltpu.VMEM)
    smem = pl.BlockSpec(memory_space=pltpu.SMEM)
    hbm = pl.BlockSpec(memory_space=pl.ANY)
    bf16, f32 = jnp.bfloat16, jnp.float32
    dma = pltpu.SemaphoreType.DMA
    return pl.pallas_call(
        kernel,
        out_shape=jax.ShapeDtypeStruct(residual_in.shape, residual_in.dtype),
        in_specs=[smem, smem, hbm, hbm, hbm],
        out_specs=vmem,
        scratch_shapes=[
            pltpu.VMEM(factor_blocks.shape, bf16),
            pltpu.VMEM(amplitudes.shape, bf16),
            pltpu.VMEM(residual_in.shape, f32),
            pltpu.SMEM((96,), jnp.int32),
            pltpu.VMEM((TV * 32, WIDE), bf16),
            pltpu.VMEM((8, CH, 2, 16, LN), bf16),
        ]
        + [pltpu.VMEM((256, 16, LN), bf16)] * CH
        + [pltpu.VMEM((32, 7, 16, LN), bf16)] * (2 * CH)
        + [
            pltpu.VMEM((WIDE, WIDE), f32),
            pltpu.VMEM((TV, 32, LN), f32),
            pltpu.VMEM((LN, WIDE), f32),
            pltpu.VMEM((CH, 16, 32, LN), bf16),
            pltpu.VMEM((CH, 16, 32, LN), bf16),
            pltpu.VMEM((2, 32, WIDE), f32),
            dma((3,)),
            dma,
            dma((CH,)),
            dma((CH,)),
            dma((CH * 32,)),
            dma((CH,)),
            dma((CH,)),
            dma,
            dma((CH,)),
        ],
        compiler_params=pltpu.CompilerParams(collective_id=0, has_side_effects=True),
    )(task_owners.T, task_local.T, factor_blocks, amplitudes, residual_in)


def solution(mesh):
    placed = (P("task", "pair", None), P("task", "pair", None), P("task", "pair", None), P(), P())
    return jax.shard_map(
        per_device, mesh=mesh, in_specs=placed, out_specs=P("task", "pair", None), check_vma=False
    )
```

time: 137 us -> 123 us (0.90)
  Pallas kernels: 130 us -> 120 us
  local copies, waits for them, and re-layouts: 3.81 us -> 1.59 us
    pallas_call x1, Pallas kernels: 130 us -> 120 us  [per_device(): pl.pallas_call(kernel, out_shape=jax.ShapeDtypeStruct(residual_in.shape,...]
where the time goes in v2:
time: 123 us; the launch traced here: 121 us
  Pallas kernels  120 us (98%)
  local copies, waits for them, and re-layouts  1.59 us (1%)
    pallas_call x1, Pallas kernels, per_device(): pl.pallas_call(kernel, out_shape=jax.ShapeDtypeStruct(residual_in.shape,...  120 us

profile of v2, /device:TPU:6, one launch (start us, length us, event | category | flops | bytes accessed | tf_op | source)
XLA Modules:
  0.0 121.1 jit_solution(8582943875152928033)
XLA Ops:
  0.0 119.5 %shard_map.55 = f32[2,32,625]{2,1,0:T(8,128)} custom-call(s32[3,512]{1,0:T(4,128)} %bitcast.2, s32[4,512]{1,0:T(4,128)} %bitcast.3, bf16[2,96,625]{2,1,0:T(8,128)(2,1)} %factor_hbm.1, bf16[2,32,625]{2,1,0:T(8,128)(2,1)} %amp_hbm.1, f32[2,32,625]{2,1,0:T(8,128)} %residual_hbm.1), custom_call_target="tpu_custom_call" | custom-call | tf_op jit(solution)/shard_map/pallas_call | solution.py:295
  119.5 1.6 %copy.7 = f32[2,32,625]{2,1,0:T(8,128)} copy(f32[2,32,625]{2,1,0:T(8,128)} %shard_map.55) | data formatting | bytes 320000

commit v3 on v2

v3 whole, which is shorter than its diff:
```python
import functools

import jax
import jax.numpy as jnp
from jax import lax
from jax.experimental import pallas as pl
from jax.experimental.pallas import tpu as pltpu
from jax.sharding import PartitionSpec as P

TV = 25
TT = 625
CH = 5
LN = 128
WIDE = CH * LN
MESH = pl.DeviceIdType.MESH
HALF_US = 0.72
HOP_US = 2.4
READY_US = 0.7
DUE_US = (15.4, 24.9, 38.1, 47.5, 49.5)


def ring_order():
    ready = {(ch, half): ch * READY_US for ch in range(CH) for half in range(2)}
    step = {key: 0 for key in ready}
    order, now = [], 0.0
    while ready:
        now = max(now, min(ready.values()))
        key = min((k for k in ready if ready[k] <= now), key=lambda k: (DUE_US[k[0]] - (8 - step[k]) * 2.9, k))
        order.append((now, key, step[key]))
        at = step[key]
        step[key] += 1
        if at == 8:
            del ready[key]
            continue
        now += HALF_US if at < 7 else HALF_US / 2
        ready[key] = now + HOP_US
    return order


def swap_matrix():
    k = lax.broadcasted_iota(jnp.int32, (TT, WIDE), 0)
    lane = lax.broadcasted_iota(jnp.int32, (TT, WIDE), 1)
    c = (k * 5243) >> 17
    d = k - c * TV
    group = (d * 13) >> 6
    target = group * LN + (d - group * 5) * TV + c
    return (lane == target).astype(jnp.float32).astype(jnp.bfloat16)


def turn_matrix():
    r = lax.broadcasted_iota(jnp.int32, (TV * 8, LN), 0)
    lane = lax.broadcasted_iota(jnp.int32, (TV * 8, LN), 1)
    d, b = r >> 3, r & 7
    target = jnp.where(b < 5, b * TV + d, -1)
    return (lane == target).astype(jnp.float32).astype(jnp.bfloat16)


def kernel(
    owners_ref, local_ref, factor_hbm, amp_hbm, residual_hbm, out_ref,
    factor_ref, amp_ref, residual_ref, base_ref, turn_ref, tiles, *more,
):
    gathered = [list(more[ch * 4 : ch * 4 + 4]) for ch in range(CH)]
    sends, recvs = more[20:25], more[25:30]
    v_ref, w_ref, l_send, l_recv, m_send, m_recv, sum_ref = more[30:37]
    (
        load_sem, spread_send, spread_recv, ring_send, ring_recv,
        plane_send, plane_recv, back_send, back_recv, last_send, last_recv,
    ) = more[37:]
    loads = [
        pltpu.make_async_copy(src, dst, load_sem.at[i])
        for i, (src, dst) in enumerate(
            ((factor_hbm, factor_ref), (amp_hbm, amp_ref), (residual_hbm, residual_ref))
        )
    ]
    for load in loads:
        load.start()

    pair = lax.axis_index("pair")
    task = lax.axis_index("task")
    y, zl = pair // 4, pair % 4
    zh, x, core = task // 8, (task // 2) % 4, task % 2
    z = zh * 4 + zl

    def place(py, pz, px, pc):
        return {"pair": py * 4 + pz % 4, "task": ((pz // 4) * 4 + px) * 2 + pc}

    right = place(y, (z + 1) % 16, x, core)
    left = place(y, (z + 15) % 16, x, core)

    def plane_peer(n):
        n = (n * 5) % 32
        return (y + n // 8) % 4, (x + (n // 2) % 4) % 4, (core + n % 2) % 2

    barrier = pltpu.get_barrier_semaphore()

    @pl.loop(1, 32)
    def _(n):
        py, px, pc = plane_peer(n)
        pl.semaphore_signal(barrier, inc=1, device_id=place(py, z, px, pc), device_id_type=MESH)

    for n in range(1, 4):
        pl.semaphore_signal(
            barrier, inc=1, device_id=place(y, zh * 4 + (zl + n) % 4, x, core), device_id_type=MESH
        )
    pl.semaphore_signal(barrier, inc=1, device_id=right, device_id_type=MESH)
    pl.semaphore_signal(barrier, inc=1, device_id=left, device_id_type=MESH)

    swap = swap_matrix()
    loads[0].wait()
    for loc in range(2):
        for ch in range(CH):
            rows = factor_ref[loc, :, ch * 125 : ch * 125 + 125]
            rows = jnp.concatenate([rows, jnp.zeros((96, 3), jnp.bfloat16)], axis=1)
            tiles[0:6, ch, loc] = rows.reshape(6, 16, LN)
    loads[1].wait()
    for loc in range(2):
        rows = jnp.dot(amp_ref[loc], swap, preferred_element_type=jnp.float32).astype(jnp.bfloat16)
        for ch in range(CH):
            tiles[6:8, ch, loc] = rows[:, ch * LN : (ch + 1) * LN].reshape(2, 16, LN)

    pl.semaphore_wait(barrier, 36)

    for ch in range(CH):
        for n in range(8):
            px, pc = (x + n // 2) % 4, (core + n % 2) % 2
            src = tiles.at[((px + 7 - zl) % 4) * 2 + pc, ch]
            dst = gathered[ch][0].at[pl.ds(zh * 16 + (x * 2 + core) * 2, 2)]
            if n == 0:
                pltpu.make_async_copy(src, dst, spread_recv.at[ch]).start()
            else:
                pltpu.make_async_remote_copy(
                    src, dst, spread_send, spread_recv.at[ch], device_id=place(y, z, px, pc), device_id_type=MESH
                ).start()

    @pl.loop(0, 32)
    def _(n):
        py, px, pc = plane_peer(n)
        k = ((zh * 4 + px) * 2 + pc) * 16 + py * 4 + zl
        for i in range(3):
            base_ref[n * 3 + i] = owners_ref[i, k] * 2 + local_ref[i, k]

    def ring_copy(ch, half, side, step, zz):
        way = -1 if side == 0 else 1
        at = pl.ds((zz // 4) * 16 + half * 8, 8)
        return pltpu.make_async_remote_copy(
            gathered[ch][(way * step) % 4].at[at], gathered[ch][(way * (step + 1)) % 4].at[at],
            ring_send.at[ch], ring_recv.at[((ch * 2 + half) * 2 + side) * 8 + step],
            device_id=right if side == 0 else left, device_id_type=MESH,
        )

    spread_done = [False] * CH

    def ring(ch, half, step):
        if step == 0 and not spread_done[ch]:
            own = gathered[ch][0].at[pl.ds(zh * 16, 16)]
            pltpu.make_async_copy(own, own, spread_recv.at[ch]).wait()
            spread_done[ch] = True
        for side in range(2):
            zz = (z + 16 - step) % 16 if side == 0 else (z + step) % 16
            if 0 < step < 8 or (step == 8 and side == half):
                ring_copy(ch, half, side, step - 1, zz).wait_recv()
            if step < 7 or (step == 7 and side == half):
                ring_copy(ch, half, side, step, zz).start()

    def plane(ch, classes):
        send, recv = sends[ch], recvs[ch]
        seat = (y * 4 + x) * 2 + core

        @pl.loop(0, 32)
        def _(n):
            row, col, amp = base_ref[n * 3], base_ref[n * 3 + 1], base_ref[n * 3 + 2]
            for q in classes:
                r = (q + zl - x + 4) % 4
                tile = ((r + 3) % 4) * 2
                send[n, tile] = gathered[ch][q][jnp.where(r == 0, amp, row)]
                send[n, tile + 1] = gathered[ch][q][col]

        def out(first, count):
            for n in range(1, 32):
                py, px, pc = plane_peer(n)
                pltpu.make_async_remote_copy(
                    send.at[n, pl.ds(first, count)], recv.at[seat, pl.ds(first, count)],
                    plane_send.at[ch], plane_recv.at[ch],
                    device_id=place(py, z, px, pc), device_id_type=MESH,
                ).start()

        for q in classes:
            r = (q + zl - x + 4) % 4

            @pl.when(r == 0)
            def _():
                out(6, 1)

            @pl.when(r != 0)
            def _():
                out(((r + 3) % 4) * 2, 2)

        if 0 in classes:
            pltpu.make_async_copy(send.at[0, pl.ds(0, 7)], recv.at[seat], plane_recv.at[ch]).start()

    def integrals(ch, kb):
        recv = recvs[ch]
        if kb == 0:
            pltpu.make_async_copy(recv, recv, plane_recv.at[ch]).wait()

        def rows_of(c, first):
            both = recvs[c][pl.ds(kb * 8, 8), 0:6].reshape(8, 3, 2, 16, LN)
            return both[:, :, first].reshape(384, LN)

        row = rows_of(ch, 0)
        cols = [rows_of(c, 1) for c in range(ch + 1)]
        part = lax.dot_general(
            row, jnp.concatenate(cols, axis=1), (((0,), (0,)), ((), ())), preferred_element_type=jnp.float32
        )
        at = (slice(ch * LN, (ch + 1) * LN), slice(0, (ch + 1) * LN))
        v_ref[at] = part if kb == 0 else v_ref[at] + part
        if ch:
            before = jnp.concatenate([rows_of(c, 0) for c in range(ch)], axis=1)
            part = lax.dot_general(before, cols[-1], (((0,), (0,)), ((), ())), preferred_element_type=jnp.float32)
            at = (slice(0, ch * LN), slice(ch * LN, (ch + 1) * LN))
            v_ref[at] = part if kb == 0 else v_ref[at] + part

    def make_turn():
        turn_ref[...] = turn_matrix()
        w_ref[...] = jnp.zeros(w_ref.shape, jnp.float32)

    lanes = lax.broadcasted_iota(jnp.int32, (8, LN), 1)

    def relay(i, j):
        part = v_ref[i * LN : (i + 1) * LN, j * LN : (j + 1) * LN].astype(jnp.bfloat16)
        turned = lax.dot_general(turn_ref[...], part, (((1,), (1,)), ((), ())), preferred_element_type=jnp.float32)
        turned = turned.reshape(TV, 8, LN)
        for g in range(CH):
            for aa in range(5):
                acc = jnp.zeros((8, LN), jnp.float32)
                for dd in range(5):
                    moved = turned[g * 5 + dd]
                    shift = ((dd - aa) * TV) % LN
                    if shift:
                        moved = pltpu.roll(moved, shift, 1)
                    acc = jnp.where((lanes >= dd * TV) & (lanes < (dd + 1) * TV), moved, acc)
                first = aa * TV + j * 5
                w_ref[i, first : first + 5, g * LN : (g + 1) * LN] = acc[:5]

    PLANE_US = 10.0
    order = ring_order()
    events = [(t, functools.partial(ring, ch, half, step)) for t, (ch, half), step in order]
    free = 0.0
    for ch in range(CH):
        reached = {n: max(t for t, (c, _), step in order if c == ch and step == n) for n in (6, 7, 8)}
        for n, classes in ((6, (2,)), (7, (1, 3)), (8, (0,))):
            events.append((reached[n] + 1e-4, functools.partial(plane, ch, classes)))
        free = max(free, reached[8]) + PLANE_US
        for kb in range(4):
            events.append((free + 4.0 + kb * 1.5, functools.partial(integrals, ch, kb)))
        if ch < CH - 1:
            for n in range(ch + 1):
                events.append((free + 9.5 + n * 0.1, functools.partial(relay, ch, n)))
                if n < ch:
                    events.append((free + 9.55 + n * 0.1, functools.partial(relay, n, ch)))
    events.append((8.0, make_turn))
    for _, event in sorted(events, key=lambda e: e[0]):
        event()

    amps = jnp.concatenate([recvs[c][:, 6].reshape(512, LN) for c in range(CH)], axis=1)

    def ladder(i):
        for j in range(CH):
            if max(i, j) == CH - 1:
                relay(i, j)
        tiles_i = lax.dot_general(
            amps, w_ref[i].astype(jnp.bfloat16), (((1,), (1,)), ((), ())), preferred_element_type=jnp.float32
        )
        l_send[i] = tiles_i.astype(jnp.bfloat16).reshape(16, 32, LN)
        dst = l_recv.at[i, y]
        for n in (1, 3, 2):
            py = (y + n) % 4
            pltpu.make_async_remote_copy(
                l_send.at[i, pl.ds(py * 4, 4)], dst, back_send, back_recv.at[i],
                device_id=place(py, z, x, core), device_id_type=MESH,
            ).start()
        pltpu.make_async_copy(l_send.at[i, pl.ds(y * 4, 4)], dst, back_recv.at[i]).start()

    def select(local, tile, loc):
        return jnp.where(local == loc, tile, 0.0)

    def fold(i):
        pltpu.make_async_copy(l_recv.at[i], l_recv.at[i], back_recv.at[i]).wait()
        locals_i = [local_ref[3, task * 16 + src * 4 + zl] for src in range(4)]
        for pz in range(4):
            got = [l_recv[i, src, pz].astype(jnp.float32) for src in range(4)]
            for loc in range(2):
                total = select(locals_i[0], got[0], loc)
                for src in range(1, 4):
                    total = total + select(locals_i[src], got[src], loc)
                m_send[i, pz, loc] = total.astype(jnp.bfloat16)
        dst = m_recv.at[i, zl]
        for n in (2, 1, 3):
            pz = (zl + n) % 4
            pltpu.make_async_remote_copy(
                m_send.at[i, pz], dst, last_send, last_recv.at[i],
                device_id=place(y, zh * 4 + pz, x, core), device_id_type=MESH,
            ).start()
        pltpu.make_async_copy(m_send.at[i, zl], dst, last_recv.at[i]).start()

    for i in range(CH + 3):
        if i < CH:
            ladder(i)
        if i >= 3:
            fold(i - 3)

    part = tiles.at[pl.ds(0, 7)]
    pltpu.make_async_copy(part, part, spread_send).wait()
    for ch in range(CH):
        part = sends[ch].at[pl.ds(0, 30)]
        pltpu.make_async_copy(part, part, ring_send.at[ch]).wait()
        part = recvs[ch].at[pl.ds(0, 31)]
        pltpu.make_async_copy(part, part, plane_send.at[ch]).wait()

    loads[2].wait()
    for i in range(CH):
        pltpu.make_async_copy(m_recv.at[i], m_recv.at[i], last_recv.at[i]).wait()
        for loc in range(2):
            total = m_recv[i, 0, loc].astype(jnp.float32)
            for src in range(1, 4):
                total = total + m_recv[i, src, loc].astype(jnp.float32)
            sum_ref[loc, :, i * LN : (i + 1) * LN] = total
    for loc in range(2):
        joined = jnp.concatenate([sum_ref[loc, :, i * LN : i * LN + 125] for i in range(CH)], axis=1)
        out_ref[loc] = residual_ref[loc] + joined
    part = l_send.at[:, pl.ds(0, 12)]
    pltpu.make_async_copy(part, part, back_send).wait()
    part = m_send.at[:, pl.ds(0, 3)]
    pltpu.make_async_copy(part, part, last_send).wait()


def per_device(factor_blocks, amplitudes, residual_in, task_owners, task_local):
    vmem = pl.BlockSpec(memory_space=pltpu.VMEM)
    smem = pl.BlockSpec(memory_space=pltpu.SMEM)
    hbm = pl.BlockSpec(memory_space=pl.ANY)
    bf16, f32 = jnp.bfloat16, jnp.float32
    dma = pltpu.SemaphoreType.DMA
    return pl.pallas_call(
        kernel,
        out_shape=jax.ShapeDtypeStruct(residual_in.shape, residual_in.dtype),
        in_specs=[smem, smem, hbm, hbm, hbm],
        out_specs=vmem,
        scratch_shapes=[
            pltpu.VMEM(factor_blocks.shape, bf16),
            pltpu.VMEM(amplitudes.shape, bf16),
            pltpu.VMEM(residual_in.shape, f32),
            pltpu.SMEM((96,), jnp.int32),
            pltpu.VMEM((TV * 8, LN), bf16),
            pltpu.VMEM((8, CH, 2, 16, LN), bf16),
        ]
        + [pltpu.VMEM((64, 16, LN), bf16)] * (4 * CH)
        + [pltpu.VMEM((32, 8, 16, LN), bf16)] * CH
        + [pltpu.VMEM((32, 7, 16, LN), bf16)] * CH
        + [
            pltpu.VMEM((WIDE, WIDE), f32),
            pltpu.VMEM((CH, LN, WIDE), f32),
            pltpu.VMEM((CH, 16, 32, LN), bf16),
            pltpu.VMEM((CH, 4, 4, 32, LN), bf16),
            pltpu.VMEM((CH, 4, 2, 32, LN), bf16),
            pltpu.VMEM((CH, 4, 2, 32, LN), bf16),
            pltpu.VMEM((2, 32, WIDE), f32),
            dma((3,)),
            dma,
            dma((CH,)),
            dma((CH,)),
            dma((CH * 32,)),
            dma((CH,)),
            dma((CH,)),
            dma,
            dma((CH,)),
            dma,
            dma((CH,)),
        ],
        compiler_params=pltpu.CompilerParams(collective_id=0, has_side_effects=True),
    )(task_owners.T, task_local.T, factor_blocks, amplitudes, residual_in)


def solution(mesh):
    placed = (P("task", "pair", None), P("task", "pair", None), P("task", "pair", None), P(), P())
    return jax.shard_map(
        per_device, mesh=mesh, in_specs=placed, out_specs=P("task", "pair", None), check_vma=False
    )
```

time: 123 us -> 115 us (0.935)
  Pallas kernels: 120 us -> 112 us
    pallas_call x1, Pallas kernels: 120 us -> 112 us  [per_device(): pl.pallas_call(kernel, out_shape=jax.ShapeDtypeStruct(residual_in.shape,...]
where the time goes in v3:
time: 115 us; the launch traced here: 114 us
  Pallas kernels  112 us (97%)
  local copies, waits for them, and re-layouts  1.59 us (1%)
    pallas_call x1, Pallas kernels, per_device(): pl.pallas_call(kernel, out_shape=jax.ShapeDtypeStruct(residual_in.shape,...  112 us

profile of v3, /device:TPU:6, one launch (start us, length us, event | category | flops | bytes accessed | tf_op | source)
XLA Modules:
  0.0 114.0 jit_solution(2447253560330657110)
XLA Ops:
  0.0 112.4 %shard_map.55 = f32[2,32,625]{2,1,0:T(8,128)} custom-call(s32[3,512]{1,0:T(4,128)} %bitcast.2, s32[4,512]{1,0:T(4,128)} %bitcast.3, bf16[2,96,625]{2,1,0:T(8,128)(2,1)} %factor_hbm.1, bf16[2,32,625]{2,1,0:T(8,128)(2,1)} %amp_hbm.1, f32[2,32,625]{2,1,0:T(8,128)} %residual_hbm.1), custom_call_target="tpu_custom_call" | custom-call | tf_op jit(solution)/shard_map/pallas_call | solution.py:343
  112.4 1.6 %copy.7 = f32[2,32,625]{2,1,0:T(8,128)} copy(f32[2,32,625]{2,1,0:T(8,128)} %shard_map.55) | data formatting | bytes 320000

commit v4 on v3

--- a/solution.py
+++ b/solution.py
@@ -88,7 +88,7 @@
     left = place(y, (z + 15) % 16, x, core)
 
     def plane_peer(n):
-        n = (n * 5) % 32
+        n = (n * 13) % 32
         return (y + n // 8) % 4, (x + (n // 2) % 4) % 4, (core + n % 2) % 2
 
     barrier = pltpu.get_barrier_semaphore()
@@ -166,14 +166,19 @@
         send, recv = sends[ch], recvs[ch]
         seat = (y * 4 + x) * 2 + core
 
-        @pl.loop(0, 32)
-        def _(n):
-            row, col, amp = base_ref[n * 3], base_ref[n * 3 + 1], base_ref[n * 3 + 2]
-            for q in classes:
-                r = (q + zl - x + 4) % 4
-                tile = ((r + 3) % 4) * 2
-                send[n, tile] = gathered[ch][q][jnp.where(r == 0, amp, row)]
-                send[n, tile + 1] = gathered[ch][q][col]
+        @pl.loop(0, 4)
+        def _(part):
+            held = []
+            for n in range(8):
+                n = part * 8 + n
+                row, col, amp = base_ref[n * 3], base_ref[n * 3 + 1], base_ref[n * 3 + 2]
+                for q in classes:
+                    r = (q + zl - x + 4) % 4
+                    tile = ((r + 3) % 4) * 2
+                    held.append((n, tile, gathered[ch][q][jnp.where(r == 0, amp, row)], gathered[ch][q][col]))
+            for n, tile, first, second in held:
+                send[n, tile] = first
+                send[n, tile + 1] = second
 
         def out(first, count):
             for n in range(1, 32):

time: 115 us -> 114 us (level)
  no operation moved by 1% of the time
where the time goes in v4:
time: 114 us
  Pallas kernels  112 us (98%)
  local copies, waits for them, and re-layouts  1.59 us (1%)
    pallas_call x1, Pallas kernels, per_device(): pl.pallas_call(kernel, out_shape=jax.ShapeDtypeStruct(residual_in.shape,...  112 us

profile of v4, /device:TPU:6, one launch (start us, length us, event | category | flops | bytes accessed | tf_op | source)
XLA Modules:
  0.0 113.8 jit_solution(4161978623623899789)
XLA Ops:
  0.0 112.2 %shard_map.55 = f32[2,32,625]{2,1,0:T(8,128)} custom-call(s32[3,512]{1,0:T(4,128)} %bitcast.2, s32[4,512]{1,0:T(4,128)} %bitcast.3, bf16[2,96,625]{2,1,0:T(8,128)(2,1)} %factor_hbm.1, bf16[2,32,625]{2,1,0:T(8,128)(2,1)} %amp_hbm.1, f32[2,32,625]{2,1,0:T(8,128)} %residual_hbm.1), custom_call_target="tpu_custom_call" | custom-call | tf_op jit(solution)/shard_map/pallas_call | solution.py:348
  112.2 1.6 %copy.7 = f32[2,32,625]{2,1,0:T(8,128)} copy(f32[2,32,625]{2,1,0:T(8,128)} %shard_map.55) | data formatting | bytes 320000
